TPU v7x, 256 devices: a whole 4x4x8 slice. The times are simulated.
256 devices in a mesh: gx: 16 (over z, core), gy: 16 (over y, x).
Axes of the slice: x: 4, y: 4, z: 8, core: 2. Of those that a mesh axis runs over, the one named last changes fastest.
Arguments:
- fine_state: float32 [9, 8, 256, 4096], P(None, None, 'gx', 'gy'), may hold values from -6 to 6
- coarse_column_state: float32 [3, 9, 12, 128, 2048], P(None, None, None, 'gx', 'gy'), may hold values from -6 to 6
- diffusivity: float32 [9], replicated, may hold values from 0.02 to 0.08
- rates: float32 [9, 9], replicated, may hold values from -0.4 to 0.4
- owner_offset: int32 [16, 16], replicated, may hold values from -1 to 1
Outputs:
- fine_new: float32 [9, 8, 256, 4096], P(None, None, 'gx', 'gy')
- coarse_new: float32 [3, 9, 12, 128, 2048], P(None, None, None, 'gx', 'gy')
Inputs may be any that keep to these rules, and one draw needn't show every extreme that they name: The coarse column over fine box (i, j) lies in slot 1 - owner_offset[i, j] of the block at gy index (j + owner_offset[i, j]) mod 16 in the same gx row; a block owns zero to three columns.
All inputs are finite; a program needn't handle non-finite values.
Results may differ from a plain program's by a relative error of at most 0.0001.
Values sent between devices are 32-bit elements; how exact they have to be, the bound alone decides.
No kernel may reach another device: no remote copies, remote signals or barrier semaphores. Data moves between devices by JAX's collectives and lax.ppermute only.
A program may use at most 128 MiB of HBM per device.

v0:
```python
import jax
import jax.numpy as jnp
from jax import lax
from jax.sharding import PartitionSpec as P

coarse_dt = 1.0
fine_dt = 0.5
fine_inv_h = 2.0
fine_inv_h2 = 4.0


def extended(block, sides, width):
    for axis, dim in sides:
        count = lax.axis_size(axis)
        forward = [(i, i + 1) for i in range(count - 1)]
        forward.append((count - 1, 0))
        backward = [(target, source) for source, target in forward]
        low = lax.ppermute(
            lax.slice_in_dim(block, block.shape[dim] - width, None, axis=dim), axis, forward
        )
        high = lax.ppermute(lax.slice_in_dim(block, 0, width, axis=dim), axis, backward)
        block = jnp.concatenate([low, block, high], axis=dim)
    return block


def passed_along(value, axis, by):
    size = lax.axis_size(axis)
    return lax.ppermute(value, axis, [(i, (i + by) % size) for i in range(size)])


def react(field, rates):
    return jnp.einsum("fg,...gzxy->...fzxy", rates, field, precision=lax.Precision.HIGHEST)


def coarse_step(column, diffusivity, rates):
    faces = -diffusivity[:, None, None, None] * (column[..., 1:, :, :] - column[..., :-1, :, :])
    zero = jnp.zeros_like(faces[..., :1, :, :])
    padded = jnp.concatenate([zero, faces, zero], axis=-3)
    change = -(padded[..., 1:, :, :] - padded[..., :-1, :, :]) + react(column, rates)
    return (column + coarse_dt * change, faces)


def spread_table(coarse_count):
    coarse_ids = lax.broadcasted_iota(jnp.int32, (coarse_count, 2 * coarse_count), 0)
    fine_ids = lax.broadcasted_iota(jnp.int32, (coarse_count, 2 * coarse_count), 1)
    return jnp.where(fine_ids // 2 == coarse_ids, 1.0, 0.0).astype(jnp.float32)


def refine(ghost):
    table = spread_table(ghost.shape[-1])
    wide = jnp.einsum("fxc,cy->fxy", ghost, table, precision=lax.Precision.HIGHEST)
    return jnp.repeat(wide, 2, axis=-2)


def coarsen(flux):
    field_count, nx, ny = flux.shape
    paired = jnp.sum(flux.reshape(field_count, nx // 2, 2, ny), axis=2)
    table = spread_table(ny // 2)
    return jnp.einsum("fxy,cy->fxc", paired, table, precision=lax.Precision.HIGHEST) * 0.25


def average(field):
    field_count, vertical_count, nx, ny = field.shape
    paired = jnp.sum(
        field.reshape(field_count, vertical_count // 2, 2, nx // 2, 2, ny), axis=(2, 4)
    )
    table = spread_table(ny // 2)
    return jnp.einsum("fzxy,cy->fzxc", paired, table, precision=lax.Precision.HIGHEST) * 0.125


def finish(advanced, faces, averaged, low_sum, high_sum):
    vertical_count = advanced.shape[1]
    nslab = averaged.shape[1]
    lower = (vertical_count - nslab) // 2
    upper = lower + nslab
    fix_low = advanced[:, lower - 1] + coarse_dt * faces[:, lower - 1] - low_sum
    fix_high = advanced[:, upper] - coarse_dt * faces[:, upper - 1] + high_sum
    return jnp.concatenate(
        [
            advanced[:, : lower - 1],
            fix_low[:, None],
            averaged,
            fix_high[:, None],
            advanced[:, upper + 1 :],
        ],
        axis=1,
    )


def bounding(column, nslab):
    vertical_count = column.shape[1]
    lower = (vertical_count - nslab) // 2
    upper = lower + nslab
    return jnp.concatenate([column[:, lower - 1 : lower], column[:, upper : upper + 1]], axis=1)


def update(field, side_sum, low, high, diffusivity, rates):
    kappa = diffusivity[:, None, None, None]
    vert = jnp.concatenate([low[:, None], field, high[:, None]], axis=1)
    near = vert[:, 2:] + vert[:, :-2] + side_sum
    return field + fine_dt * (fine_inv_h2 * kappa * (near - 6.0 * field) + react(field, rates))


def edge_sides(field, padded):
    nx = field.shape[2]
    ny = field.shape[3]
    row_ids = lax.broadcasted_iota(jnp.int32, field.shape, 2)
    col_ids = lax.broadcasted_iota(jnp.int32, field.shape, 3)
    west_edge = padded[:, :, 0:1, 1 : ny + 1]
    east_edge = padded[:, :, nx + 1 : nx + 2, 1 : ny + 1]
    south_edge = padded[:, :, 1 : nx + 1, 0:1]
    north_edge = padded[:, :, 1 : nx + 1, ny + 1 : ny + 2]
    west = jnp.where(row_ids == 0, west_edge, jnp.roll(field, 1, 2))
    east = jnp.where(row_ids == nx - 1, east_edge, jnp.roll(field, -1, 2))
    south = jnp.where(col_ids == 0, south_edge, jnp.roll(field, 1, 3))
    north = jnp.where(col_ids == ny - 1, north_edge, jnp.roll(field, -1, 3))
    return east + west + (north + south)


def face_fluxes(field, low, high, diffusivity):
    flux_low = -fine_inv_h * diffusivity[:, None, None] * (field[:, 0] - low)
    flux_high = -fine_inv_h * diffusivity[:, None, None] * (high - field[:, -1])
    return (flux_low, flux_high)


def fine_part(fine_state, rim_old, rim_new, diffusivity, rates):
    rim_mid = 0.5 * (rim_old + rim_new)
    field = fine_state
    total_low = jnp.zeros(fine_state.shape[0:1] + fine_state.shape[2:], jnp.float32)
    total_high = jnp.zeros(fine_state.shape[0:1] + fine_state.shape[2:], jnp.float32)
    for ghosts in (rim_old, rim_mid):
        low = refine(ghosts[:, 0])
        high = refine(ghosts[:, 1])
        padded = extended(field, (("gx", 2), ("gy", 3)), 1)
        flux_low, flux_high = face_fluxes(field, low, high, diffusivity)
        field = update(field, edge_sides(field, padded), low, high, diffusivity, rates)
        total_low = total_low + fine_dt * flux_low
        total_high = total_high + fine_dt * flux_high
    payload = (average(field), coarsen(total_low), coarsen(total_high))
    return (field, payload)


def on_device(fine_state, coarse_column_state, diffusivity, rates, owner_offset):
    row_index = lax.axis_index("gx")
    col_index = lax.axis_index("gy")
    across = lax.axis_size("gy")
    mine = owner_offset[row_index, col_index]
    left_used = owner_offset[row_index, (col_index + across - 1) % across] == 1
    self_used = mine == 0
    right_used = owner_offset[row_index, (col_index + 1) % across] == -1
    nslab = fine_state.shape[1] // 2

    def select(from_left, own, from_right):
        return jnp.where(mine == -1, from_left, jnp.where(mine == 1, from_right, own))

    advanced, faces = coarse_step(coarse_column_state, diffusivity, rates)
    left_rims = passed_along(
        (bounding(coarse_column_state[2], nslab), bounding(advanced[2], nslab)), "gy", 1
    )
    right_rims = passed_along(
        (bounding(coarse_column_state[0], nslab), bounding(advanced[0], nslab)), "gy", -1
    )
    rim_old = select(left_rims[0], bounding(coarse_column_state[1], nslab), right_rims[0])
    rim_new = select(left_rims[1], bounding(advanced[1], nslab), right_rims[1])
    fine_new, payload = fine_part(fine_state, rim_old, rim_new, diffusivity, rates)
    toward_left = passed_along((payload[0], payload[1], payload[2]), "gy", -1)
    toward_right = passed_along((payload[0], payload[1], payload[2]), "gy", 1)
    slot_zero = jnp.where(
        left_used, finish(advanced[0], faces[0], *toward_right), coarse_column_state[0]
    )
    slot_one = jnp.where(self_used, finish(advanced[1], faces[1], *payload), coarse_column_state[1])
    slot_two = jnp.where(
        right_used, finish(advanced[2], faces[2], *toward_left), coarse_column_state[2]
    )
    return (fine_new, jnp.stack([slot_zero, slot_one, slot_two], axis=0))


def solution(mesh):
    in_specs = (P(None, None, "gx", "gy"), P(None, None, None, "gx", "gy"), P(), P(), P())
    out_specs = (P(None, None, "gx", "gy"), P(None, None, None, "gx", "gy"))
    return jax.shard_map(
        on_device, mesh=mesh, in_specs=in_specs, out_specs=out_specs, check_vma=False
    )
```

profile of v0, /device:TPU:0, one launch (start us, length us, event | category | flops | bytes accessed | tf_op | source)
XLA Modules:
  0.0 175.6 jit_solution(18181004273895627498)
XLA Ops:
  1.4 1.9 %fusion.23 = f32[3,9,11,8,128]{4,3,1,2,0:T(8,128)S(1)} fusion(f32[9]{0:T(128)S(1)} %get-tuple-element.77, f32[3,9,12,8,128]{4,3,2,1,0:T(8,128)} %param.6), kind=kLoop, calls=%fused_computation.39 | loop fusion | flops 608256 | bytes 3649572 | tf_op jit(solution)/shard_map/mul | solution.py:36
  3.3 3.2 %fusion = f32[3,12,8,128,9]{3,4,2,1,0:T(8,128)S(1)} fusion(f32[3,9,12,8,128]{4,3,2,1,0:T(8,128)S(1)} %copy-done.2, f32[9,9]{1,0:T(8,128)S(1)} %copy-done), kind=kOutput, calls=%fused_computation.1 | convolution fusion | flops 35831808 | bytes 2654532 | tf_op jit(solution)/shard_map/fg,...gzxy->...fzxy/dot_general | solution.py:32
  8.8 3.5 %collective-permute-start.7 = (f32[9,2,8,128]{3,2,0,1:T(8,128)}, f32[9,2,8,128]{3,2,0,1:T(8,128)S(1)}, u32[]{:S(2)}, u32[]{:S(2)}) collective-permute-start(f32[9,2,8,128]{3,2,0,1:T(8,128)} %pad_maximum_fusion.9), channel_id=1, source_target_pairs={{0,15},{1,0},{2,1},{3,2},{4,3},{5,4},{6,5},{7,6},{8,7},{9,8},{10,9... | collective-permute-start | bytes 221192 | tf_op jit(solution)/shard_map/ppermute | solution.py:28
  15.1 5.3 %collective-permute-start.1 = (f32[9,2,8,128]{3,2,0,1:T(8,128)}, f32[9,2,8,128]{3,2,0,1:T(8,128)}, u32[]{:S(2)}, u32[]{:S(2)}) collective-permute-start(f32[9,2,8,128]{3,2,0,1:T(8,128)} %pad_maximum_fusion.7), channel_id=1, source_target_pairs={{0,15},{1,0},{2,1},{3,2},{4,3},{5,4},{6,5},{7,6},{8,7},{9,8},{10,9... | collective-permute-start | bytes 221192 | tf_op jit(solution)/shard_map/ppermute | solution.py:28
  22.0 6.5 %copy.138 = f32[9,8,16,256]{2,1,0,3:T(8,128)} copy(f32[9,8,16,256]{3,2,1,0:T(8,128)} %param.5) | data formatting | bytes 2359296 | tf_op args[0]
  28.5 2.8 %fusion.138 = (f32[9,8,16,255]{3,0,2,1:T(8,128)}, f32[9,8,16,255]{3,0,2,1:T(8,128)}) fusion(f32[9,8,16,256]{3,0,2,1:T(8,128)S(1)} %copy.148), kind=kLoop, calls=%fused_computation.212 | loop fusion | bytes 4700160 | tf_op jit(solution)/shard_map/jit(_roll_static)/slice | solution.py:115
  31.3 2.4 %fusion.140 = (f32[9,8,15,256]{3,0,2,1:T(8,128)}, f32[9,8,15,256]{3,0,2,1:T(8,128)}) fusion(f32[9,8,16,256]{3,0,2,1:T(8,128)S(1)} %copy.148), kind=kLoop, calls=%fused_computation.214 | loop fusion | bytes 4423680 | tf_op jit(solution)/shard_map/jit(_roll_static)/slice | solution.py:113
  50.3 4.5 %collective-permute-start.2 = (f32[9,8,1,256]{3,0,2,1:T(8,128)S(1)}, f32[9,8,1,256]{3,0,2,1:T(8,128)S(1)}, u32[]{:S(2)}, u32[]{:S(2)}) collective-permute-start(f32[9,8,1,256]{3,0,2,1:T(8,128)S(1)} %copy-done.23), channel_id=1, source_target_pairs={{16,0},{32,16},{48,32},{64,48},{80,64},{96,80},{112,96},{128,112},... | collective-permute-start | bytes 221192 | tf_op jit(solution)/shard_map/ppermute | solution.py:21
  55.4 13.6 %copy.137 = f32[9,8,1,256]{2,1,0,3:T(8,128)} copy(f32[9,8,1,256]{3,0,2,1:T(8,128)} %collective-permute-done.3) | data formatting | bytes 147456 | tf_op jit(solution)/shard_map/ppermute | solution.py:18
  69.1 12.9 %copy.139 = f32[9,8,1,256]{2,1,0,3:T(8,128)} copy(f32[9,8,1,256]{3,0,2,1:T(8,128)S(1)} %collective-permute-done.2) | data formatting | bytes 147456 | tf_op jit(solution)/shard_map/ppermute | solution.py:21
  82.9 2.7 %collective-permute-start.4 = (f32[9,8,18,1]{2,1,0,3:T(8,128)S(1)}, f32[9,8,18,1]{2,1,0,3:T(8,128)S(1)}, u32[]{:S(2)}, u32[]{:S(2)}) collective-permute-start(f32[9,8,18,1]{2,1,0,3:T(8,128)S(1)} %get-tuple-element.20), channel_id=1, source_target_pairs={{1,0},{2,1},{3,2},{4,3},{5,4},{6,5},{7,6},{8,7},{9,8},{10,9},{11,1... | collective-permute-start | bytes 15560 | tf_op jit(solution)/shard_map/ppermute | solution.py:21
  87.6 5.2 %collective-permute-done.5 = f32[9,8,18,1]{2,1,0,3:T(8,128)S(1)} collective-permute-done((f32[9,8,18,1]{2,1,0,3:T(8,128)S(1)}, f32[9,8,18,1]{2,1,0,3:T(8,128)S(1)}, u32[]{:S(2)}, u32[]{:S(2)}) %collective-permute-start.5) | collective-permute-done | bytes 5216 | tf_op jit(solution)/shard_map/ppermute | solution.py:18
  93.8 9.3 %fusion.15 = f32[9,8,16,256]{3,0,2,1:T(8,128)S(1)} fusion(f32[9,8,16,256]{3,0,2,1:T(8,128)} %copy-done.1, f32[9,1,16,256]{3,0,2,1:T(8,128)S(1)} %bitcast.201, f32[9,1,16,256]{3,0,2,1:T(8,128)S(1)} %bitcast.200, f32[9,8,1,256]{3,0,2,1:T(8,128)} %get-tuple-element.39, f32[9,8,15,256]{3,0,2,1:T(8,128)} %get-tuple-element.41, ...), kind=kOutput, calls=%fused_computation.19 | convolution fusion | flops 38043648 | bytes 8710024 | tf_op jit(solution)/shard_map/fg,...gzxy->...fzxy/dot_general | solution.py:32
  103.2 2.8 %fusion.134 = (f32[9,8,16,255]{3,0,2,1:T(8,128)}, f32[9,8,16,255]{3,0,2,1:T(8,128)}) fusion(f32[9,8,16,256]{3,0,2,1:T(8,128)S(1)} %fusion.15), kind=kLoop, calls=%fused_computation.208 | loop fusion | bytes 4700160 | tf_op jit(solution)/shard_map/jit(_roll_static)/slice | solution.py:115
  106.0 2.6 %fusion.136 = (f32[9,8,15,256]{3,0,2,1:T(8,128)}, f32[9,8,15,256]{3,0,2,1:T(8,128)}) fusion(f32[9,8,16,256]{3,0,2,1:T(8,128)S(1)} %fusion.15), kind=kLoop, calls=%fused_computation.210 | loop fusion | bytes 4423680 | tf_op jit(solution)/shard_map/jit(_roll_static)/slice | solution.py:113
  118.0 2.1 %collective-permute-done.9 = f32[9,8,1,256]{3,0,2,1:T(8,128)S(1)} collective-permute-done((f32[9,8,1,256]{3,0,2,1:T(8,128)S(1)}, f32[9,8,1,256]{3,0,2,1:T(8,128)S(1)}, u32[]{:S(2)}, u32[]{:S(2)}) %collective-permute-start.9) | collective-permute-done | bytes 73760 | tf_op jit(solution)/shard_map/ppermute | solution.py:18
  124.3 4.1 %collective-permute-start.10 = (f32[9,8,18,1]{2,1,3,0:T(8,128)S(1)}, f32[9,8,18,1]{2,1,3,0:T(8,128)}, u32[]{:S(2)}, u32[]{:S(2)}) collective-permute-start(f32[9,8,18,1]{2,1,3,0:T(8,128)S(1)} %copy.156), channel_id=1, source_target_pairs={{1,0},{2,1},{3,2},{4,3},{5,4},{6,5},{7,6},{8,7},{9,8},{10,9},{11,1... | collective-permute-start | bytes 15560 | tf_op jit(solution)/shard_map/ppermute | solution.py:21
  129.9 2.4 %copy.159 = f32[9,8,18,1]{2,1,3,0:T(8,128)} copy(f32[9,8,18,1]{3,0,2,1:T(8,128)} %get-tuple-element.23) | data formatting | bytes 10368 | tf_op jit(solution)/shard_map/slice | solution.py:19
  133.9 6.0 %collective-permute-done.11 = f32[9,8,18,1]{2,1,3,0:T(8,128)} collective-permute-done((f32[9,8,18,1]{2,1,3,0:T(8,128)}, f32[9,8,18,1]{2,1,3,0:T(8,128)}, u32[]{:S(2)}, u32[]{:S(2)}) %collective-permute-start.11) | collective-permute-done | bytes 5216 | tf_op jit(solution)/shard_map/ppermute | solution.py:18
  143.3 7.6 %fusion.8 = f32[9,8,16,256]{3,0,2,1:T(8,128)} fusion(f32[9,8,16,256]{3,0,2,1:T(8,128)S(1)} %fusion.15, f32[9,1,16,256]{3,0,2,1:T(8,128)S(1)} %bitcast.199, f32[9,1,16,256]{3,0,2,1:T(8,128)S(1)} %bitcast.198, f32[9,8,1,256]{3,0,2,1:T(8,128)} %copy-done.25, f32[9,8,15,256]{3,0,2,1:T(8,128)} %get-tuple-element.33, f32[9,8,15,256]{3,0,2,1:T(8,128)} %get-tuple-element.32, ...), kind=kOutput, calls=%fused_computation.10 | convolution fusion | flops 38043648 | bytes 7530376 | tf_op jit(solution)/shard_map/fg,...gzxy->...fzxy/dot_general | solution.py:32
  151.0 2.8 %reduce_sum.28 = f32[9,4,8,256]{3,0,2,1:T(8,128)} reduce(f32[9,4,2,8,2,256]{5,0,4,3,2,1:T(8,128)} %bitcast.193, f32[]{:T(128)} %constant.80.clone.1), dimensions={2,4}, to_apply=%region_1.2 | reduce | flops 221184 | bytes 1474564 | tf_op jit(solution)/shard_map/reduce_sum | solution.py:64
  157.6 2.0 %collective-permute-start.14 = (f32[9,8,128]{2,1,0:T(8,128)S(1)}, f32[9,8,128]{2,1,0:T(8,128)S(1)}, u32[]{:S(2)}, u32[]{:S(2)}) collective-permute-start(f32[9,8,128]{2,1,0:T(8,128)S(1)} %get-tuple-element.13), channel_id=1, source_target_pairs={{0,1},{1,2},{2,3},{3,4},{4,5},{5,6},{6,7},{7,8},{8,9},{9,10},{10,1... | collective-permute-start | bytes 110600 | tf_op jit(solution)/shard_map/ppermute | solution.py:28
  159.7 3.3 %collective-permute-start.16 = (f32[9,4,8,128]{3,2,0,1:T(8,128)S(1)}, f32[9,4,8,128]{3,2,0,1:T(8,128)S(1)}, u32[]{:S(2)}, u32[]{:S(2)}) collective-permute-start(f32[9,4,8,128]{3,2,0,1:T(8,128)S(1)} %get-tuple-element.15), channel_id=1, source_target_pairs={{0,15},{1,0},{2,1},{3,2},{4,3},{5,4},{6,5},{7,6},{8,7},{9,8},{10,9... | collective-permute-start | bytes 442376 | tf_op jit(solution)/shard_map/ppermute | solution.py:28
  166.5 5.0 %collective-permute-done.13 = f32[9,4,8,128]{3,2,0,1:T(8,128)S(1)} collective-permute-done((f32[9,4,8,128]{3,2,0,1:T(8,128)S(1)}, f32[9,4,8,128]{3,2,0,1:T(8,128)S(1)}, u32[]{:S(2)}, u32[]{:S(2)}) %collective-permute-start.13) | collective-permute-done | bytes 147488 | tf_op jit(solution)/shard_map/ppermute | solution.py:28
  (151 shorter events, 56.8 us)
Async XLA Ops:
  8.8 41.5 %collective-permute-start.7 = (f32[9,2,8,128]{3,2,0,1:T(8,128)}, f32[9,2,8,128]{3,2,0,1:T(8,128)S(1)}, u32[]{:S(2)}, u32[]{:S(2)}) collective-permute-start(f32[9,2,8,128]{3,2,0,1:T(8,128)} %pad_maximum_fusion.9), channel_id=1, source_target_pairs={{0,15},{1,0},{2,1},{3,2},{4,3},{5,4},{6,5},{7,6},{8,7},{9,8},{10,9... | collective-permute-start | bytes 221192 | tf_op jit(solution)/shard_map/ppermute | solution.py:28
  12.9 41.9 %collective-permute-start.6 = (f32[9,2,8,128]{3,2,0,1:T(8,128)}, f32[9,2,8,128]{3,2,0,1:T(8,128)}, u32[]{:S(2)}, u32[]{:S(2)}) collective-permute-start(f32[9,2,8,128]{3,2,0,1:T(8,128)} %pad_maximum_fusion.8), channel_id=1, source_target_pairs={{0,1},{1,2},{2,3},{3,4},{4,5},{5,6},{6,7},{7,8},{8,9},{9,10},{10,1... | collective-permute-start | bytes 221192 | tf_op jit(solution)/shard_map/ppermute | solution.py:28
  14.5 40.3 %collective-permute-start = (f32[9,2,8,128]{3,2,0,1:T(8,128)}, f32[9,2,8,128]{3,2,0,1:T(8,128)}, u32[]{:S(2)}, u32[]{:S(2)}) collective-permute-start(f32[9,2,8,128]{3,2,0,1:T(8,128)} %pad_maximum_fusion.6), channel_id=1, source_target_pairs={{0,1},{1,2},{2,3},{3,4},{4,5},{5,6},{6,7},{7,8},{8,9},{9,10},{10,1... | collective-permute-start | bytes 221192 | tf_op jit(solution)/shard_map/ppermute | solution.py:28
  15.1 39.7 %collective-permute-start.1 = (f32[9,2,8,128]{3,2,0,1:T(8,128)}, f32[9,2,8,128]{3,2,0,1:T(8,128)}, u32[]{:S(2)}, u32[]{:S(2)}) collective-permute-start(f32[9,2,8,128]{3,2,0,1:T(8,128)} %pad_maximum_fusion.7), channel_id=1, source_target_pairs={{0,15},{1,0},{2,1},{3,2},{4,3},{5,4},{6,5},{7,6},{8,7},{9,8},{10,9... | collective-permute-start | bytes 221192 | tf_op jit(solution)/shard_map/ppermute | solution.py:28
  22.0 33.4 %collective-permute-start.3 = (f32[9,8,1,256]{3,0,2,1:T(8,128)}, f32[9,8,1,256]{3,0,2,1:T(8,128)}, u32[]{:S(2)}, u32[]{:S(2)}) collective-permute-start(f32[9,8,1,256]{3,0,2,1:T(8,128)} %get-tuple-element.38), channel_id=1, source_target_pairs={{0,16},{16,32},{32,48},{48,64},{64,80},{80,96},{96,112},{112,128},... | collective-permute-start | bytes 221192 | tf_op jit(solution)/shard_map/ppermute | solution.py:18
  37.6 12.7 %copy-start.23 = (f32[9,8,1,256]{3,0,2,1:T(8,128)S(1)}, f32[9,8,1,256]{3,0,2,1:T(8,128)}, u32[]{:S(2)}) copy-start(f32[9,8,1,256]{3,0,2,1:T(8,128)} %get-tuple-element.39) | copy-start | bytes 221188
  50.3 18.7 %collective-permute-start.2 = (f32[9,8,1,256]{3,0,2,1:T(8,128)S(1)}, f32[9,8,1,256]{3,0,2,1:T(8,128)S(1)}, u32[]{:S(2)}, u32[]{:S(2)}) collective-permute-start(f32[9,8,1,256]{3,0,2,1:T(8,128)S(1)} %copy-done.23), channel_id=1, source_target_pairs={{16,0},{32,16},{48,32},{64,48},{80,64},{96,80},{112,96},{128,112},... | collective-permute-start | bytes 221192 | tf_op jit(solution)/shard_map/ppermute | solution.py:21
  55.1 38.6 %copy-start.11 = (f32[9,8,256]{2,0,1:T(8,128)}, f32[9,8,256]{2,0,1:T(8,128)S(1)}, u32[]{:S(2)}) copy-start(f32[9,8,256]{2,0,1:T(8,128)S(1)} %fusion.35) | copy-start | bytes 221188
  55.4 38.3 %copy-start.13 = (f32[9,8,256]{2,0,1:T(8,128)}, f32[9,8,256]{2,0,1:T(8,128)S(1)}, u32[]{:S(2)}) copy-start(f32[9,8,256]{2,0,1:T(8,128)S(1)} %fusion.34) | copy-start | bytes 221188
  69.1 12.9 %copy-start.20 = (f32[9,8,1,256]{3,0,2,1:T(8,128)}, f32[9,8,1,256]{3,0,2,1:T(8,128)S(1)}, u32[]{:S(2)}) copy-start(f32[9,8,1,256]{3,0,2,1:T(8,128)S(1)} %collective-permute-done.2) | copy-start | bytes 221188
  82.9 4.5 %collective-permute-start.4 = (f32[9,8,18,1]{2,1,0,3:T(8,128)S(1)}, f32[9,8,18,1]{2,1,0,3:T(8,128)S(1)}, u32[]{:S(2)}, u32[]{:S(2)}) collective-permute-start(f32[9,8,18,1]{2,1,0,3:T(8,128)S(1)} %get-tuple-element.20), channel_id=1, source_target_pairs={{1,0},{2,1},{3,2},{4,3},{5,4},{6,5},{7,6},{8,7},{9,8},{10,9},{11,1... | collective-permute-start | bytes 15560 | tf_op jit(solution)/shard_map/ppermute | solution.py:21
  85.6 7.3 %collective-permute-start.5 = (f32[9,8,18,1]{2,1,0,3:T(8,128)S(1)}, f32[9,8,18,1]{2,1,0,3:T(8,128)S(1)}, u32[]{:S(2)}, u32[]{:S(2)}) collective-permute-start(f32[9,8,18,1]{2,1,0,3:T(8,128)S(1)} %get-tuple-element.21), channel_id=1, source_target_pairs={{0,1},{1,2},{2,3},{3,4},{4,5},{5,6},{6,7},{7,8},{8,9},{9,10},{10,1... | collective-permute-start | bytes 15560 | tf_op jit(solution)/shard_map/ppermute | solution.py:18
  112.4 4.2 %collective-permute-start.15 = (f32[9,8,128]{2,1,0:T(8,128)}, f32[9,8,128]{2,1,0:T(8,128)S(1)}, u32[]{:S(2)}, u32[]{:S(2)}) collective-permute-start(f32[9,8,128]{2,1,0:T(8,128)} %get-tuple-element.17), channel_id=1, source_target_pairs={{0,15},{1,0},{2,1},{3,2},{4,3},{5,4},{6,5},{7,6},{8,7},{9,8},{10,9... | collective-permute-start | bytes 110600 | tf_op jit(solution)/shard_map/ppermute | solution.py:28
  112.6 15.8 %collective-permute-start.12 = (f32[9,8,128]{2,1,0:T(8,128)}, f32[9,8,128]{2,1,0:T(8,128)}, u32[]{:S(2)}, u32[]{:S(2)}) collective-permute-start(f32[9,8,128]{2,1,0:T(8,128)} %get-tuple-element.17), channel_id=1, source_target_pairs={{0,1},{1,2},{2,3},{3,4},{4,5},{5,6},{6,7},{7,8},{8,9},{9,10},{10,1... | collective-permute-start | bytes 110600 | tf_op jit(solution)/shard_map/ppermute | solution.py:28
  114.4 3.6 %collective-permute-start.8 = (f32[9,8,1,256]{3,0,2,1:T(8,128)S(1)}, f32[9,8,1,256]{3,0,2,1:T(8,128)S(1)}, u32[]{:S(2)}, u32[]{:S(2)}) collective-permute-start(f32[9,8,1,256]{3,0,2,1:T(8,128)S(1)} %get-tuple-element.31), channel_id=1, source_target_pairs={{16,0},{32,16},{48,32},{64,48},{80,64},{96,80},{112,96},{128,112},... | collective-permute-start | bytes 221192 | tf_op jit(solution)/shard_map/ppermute | solution.py:21
  114.4 5.6 %collective-permute-start.9 = (f32[9,8,1,256]{3,0,2,1:T(8,128)S(1)}, f32[9,8,1,256]{3,0,2,1:T(8,128)S(1)}, u32[]{:S(2)}, u32[]{:S(2)}) collective-permute-start(f32[9,8,1,256]{3,0,2,1:T(8,128)S(1)} %get-tuple-element.30), channel_id=1, source_target_pairs={{0,16},{16,32},{32,48},{48,64},{64,80},{80,96},{96,112},{112,128},... | collective-permute-start | bytes 221192 | tf_op jit(solution)/shard_map/ppermute | solution.py:18
  122.5 20.8 %copy-start.26 = (pred[256]{0:T(512)(128)(4,1)S(1)}, pred[256]{0:T(512)(128)(4,1)}, u32[]{:S(2)}) copy-start(pred[256]{0:T(512)(128)(4,1)} %get-tuple-element.86) | copy-start | bytes 772
  124.3 8.0 %collective-permute-start.10 = (f32[9,8,18,1]{2,1,3,0:T(8,128)S(1)}, f32[9,8,18,1]{2,1,3,0:T(8,128)}, u32[]{:S(2)}, u32[]{:S(2)}) collective-permute-start(f32[9,8,18,1]{2,1,3,0:T(8,128)S(1)} %copy.156), channel_id=1, source_target_pairs={{1,0},{2,1},{3,2},{4,3},{5,4},{6,5},{7,6},{8,7},{9,8},{10,9},{11,1... | collective-permute-start | bytes 15560 | tf_op jit(solution)/shard_map/ppermute | solution.py:21
  132.3 7.6 %collective-permute-start.11 = (f32[9,8,18,1]{2,1,3,0:T(8,128)}, f32[9,8,18,1]{2,1,3,0:T(8,128)}, u32[]{:S(2)}, u32[]{:S(2)}) collective-permute-start(f32[9,8,18,1]{2,1,3,0:T(8,128)} %copy.159), channel_id=1, source_target_pairs={{0,1},{1,2},{2,3},{3,4},{4,5},{5,6},{6,7},{7,8},{8,9},{9,10},{10,1... | collective-permute-start | bytes 15560 | tf_op jit(solution)/shard_map/ppermute | solution.py:18
  156.1 15.3 %copy-start.17 = (f32[1,9,12,8,128]{4,3,1,2,0:T(8,128)S(1)}, f32[1,9,12,8,128]{4,3,1,2,0:T(8,128)}, u32[]{:S(2)}) copy-start(f32[1,9,12,8,128]{4,3,1,2,0:T(8,128)} %fusion.109) | copy-start | bytes 1327108
  157.6 8.0 %collective-permute-start.17 = (f32[9,8,128]{2,1,0:T(8,128)S(1)}, f32[9,8,128]{2,1,0:T(8,128)S(1)}, u32[]{:S(2)}, u32[]{:S(2)}) collective-permute-start(f32[9,8,128]{2,1,0:T(8,128)S(1)} %get-tuple-element.13), channel_id=1, source_target_pairs={{0,15},{1,0},{2,1},{3,2},{4,3},{5,4},{6,5},{7,6},{8,7},{9,8},{10,9... | collective-permute-start | bytes 110600 | tf_op jit(solution)/shard_map/ppermute | solution.py:28
  157.6 14.7 %collective-permute-start.14 = (f32[9,8,128]{2,1,0:T(8,128)S(1)}, f32[9,8,128]{2,1,0:T(8,128)S(1)}, u32[]{:S(2)}, u32[]{:S(2)}) collective-permute-start(f32[9,8,128]{2,1,0:T(8,128)S(1)} %get-tuple-element.13), channel_id=1, source_target_pairs={{0,1},{1,2},{2,3},{3,4},{4,5},{5,6},{6,7},{7,8},{8,9},{9,10},{10,1... | collective-permute-start | bytes 110600 | tf_op jit(solution)/shard_map/ppermute | solution.py:28
  159.7 6.0 %collective-permute-start.16 = (f32[9,4,8,128]{3,2,0,1:T(8,128)S(1)}, f32[9,4,8,128]{3,2,0,1:T(8,128)S(1)}, u32[]{:S(2)}, u32[]{:S(2)}) collective-permute-start(f32[9,4,8,128]{3,2,0,1:T(8,128)S(1)} %get-tuple-element.15), channel_id=1, source_target_pairs={{0,15},{1,0},{2,1},{3,2},{4,3},{5,4},{6,5},{7,6},{8,7},{9,8},{10,9... | collective-permute-start | bytes 442376 | tf_op jit(solution)/shard_map/ppermute | solution.py:28
  163.0 8.5 %collective-permute-start.13 = (f32[9,4,8,128]{3,2,0,1:T(8,128)S(1)}, f32[9,4,8,128]{3,2,0,1:T(8,128)S(1)}, u32[]{:S(2)}, u32[]{:S(2)}) collective-permute-start(f32[9,4,8,128]{3,2,0,1:T(8,128)S(1)} %get-tuple-element.15), channel_id=1, source_target_pairs={{0,1},{1,2},{2,3},{3,4},{4,5},{5,6},{6,7},{7,8},{8,9},{9,10},{10,1... | collective-permute-start | bytes 442376 | tf_op jit(solution)/shard_map/ppermute | solution.py:28
  (21 other events, 116.7 us)
where the time goes:
time: 177 us; the launch traced here: 176 us
  local copies, waits for them, and re-layouts  79.2 us (45%)
  starting transfers between devices  28.1 us (16%)
  matrix products  24.6 us (14%)
  other arithmetic  19.8 us (11%)
  waiting for transfers between devices  19.7 us (11%)
  between operations  4.22 us (2%)
    dot_general x3, matrix products, react(): jnp.einsum('fg,...gzxy->...fzxy', rates, field, precision=lax.Precision.H...  20.1 us
    ppermute x10, starting transfers between devices, passed_along(): lax.ppermute(value, axis, [(i, (i + by) % size) for i in range(size)])  16.2 us
    unnamed x63, local copies, waits for them, and re-layouts  15.3 us
    ppermute x1, local copies, waits for them, and re-layouts, extended(): lax.ppermute(lax.slice_in_dim(block, block.shape[dim] - width, None, axis...  13.6 us
    ppermute x4, waiting for transfers between devices, extended(): lax.ppermute(lax.slice_in_dim(block, block.shape[dim] - width, None, axis...  13.3 us
    ppermute x1, local copies, waits for them, and re-layouts, extended(): lax.ppermute(lax.slice_in_dim(block, 0, width, axis=dim), axis, backward)  12.9 us
    ppermute x4, starting transfers between devices, extended(): lax.ppermute(lax.slice_in_dim(block, 0, width, axis=dim), axis, backward)  11.3 us
    slice x4, local copies, waits for them, and re-layouts, edge_sides(): south = jnp.where(col_ids == 0, south_edge, jnp.roll(field, 1, 3))  9.05 us
  transfers between devices with their start and end apart: 18, of which 6 were waited for; matrix products, arithmetic and copies ran while one was open for 35% of the time, Pallas kernels for 0%

commit v1 on v0

v1 whole, which is shorter than its diff:
```python
import jax
import jax.numpy as jnp
from jax import lax
from jax.experimental import pallas as pl
from jax.experimental.pallas import tpu as pltpu
from jax.sharding import PartitionSpec as P

F32 = jnp.float32
BF16 = jnp.bfloat16
NF = 9
NZ = 8
NX = 16
NY = 256
LOW = 3
HIGH = 8
VMEM = pltpu.VMEM
SMEM = pltpu.SMEM


def call(kernel, name, outs, spaces, flops, limit=8, aliases=None, scratch=(), out_spaces=None):
    return pl.pallas_call(
        kernel,
        name=name,
        out_shape=[jax.ShapeDtypeStruct(s, F32) for s in outs],
        in_specs=[pl.BlockSpec(memory_space=s) for s in spaces],
        out_specs=[pl.BlockSpec(memory_space=s) for s in out_spaces or [VMEM] * len(outs)],
        scratch_shapes=list(scratch),
        input_output_aliases=aliases or {},
        compiler_params=pltpu.CompilerParams(vmem_limit_bytes=limit << 20),
        cost_estimate=pl.CostEstimate(flops=flops, bytes_accessed=1 << 20, transcendentals=0),
    )


def spread_table():
    coarse = lax.broadcasted_iota(jnp.int32, (128, 256), 0)
    fine = lax.broadcasted_iota(jnp.int32, (128, 256), 1)
    return jnp.where(lax.shift_right_logical(fine, 1) == coarse, 1.0, 0.0).astype(BF16)


def gather_table():
    fine = lax.broadcasted_iota(jnp.int32, (256, 128), 0)
    coarse = lax.broadcasted_iota(jnp.int32, (256, 128), 1)
    return jnp.where(lax.shift_right_logical(fine, 1) == coarse, 1.0, 0.0).astype(BF16)


def table_dot(value, table):
    high = value.astype(BF16)
    low = (value - high.astype(F32)).astype(BF16)
    return jnp.dot(high, table, preferred_element_type=F32) + jnp.dot(
        low, table, preferred_element_type=F32
    )


def reacted(tiles, f, scale, diagonal, rates):
    total = tiles[f] * (diagonal + scale * rates[f, f])
    for g in range(NF):
        if g != f:
            total = total + tiles[g] * (scale * rates[f, g])
    return total


def pack_columns(ref, side):
    lane = lax.broadcasted_iota(jnp.int32, (NX, 128), 1)
    packed = jnp.zeros((NX, 128), F32)
    for z in range(NZ):
        for f in range(NF):
            at = z * 16 + f
            tile = ref[f, side, z * NX : (z + 1) * NX, :]
            shift = at if side == 0 else (at - 127) % 128
            moved = pltpu.roll(tile, shift, 1) if shift else tile
            packed = jnp.where(lane == at, moved, packed)
    return packed


def kappa_lanes(kap):
    lane = lax.broadcasted_iota(jnp.int32, (NX, 128), 1) & 15
    out = jnp.zeros((NX, 128), F32)
    for f in range(NF):
        out = jnp.where(lane == f, 2.0 * kap[f], out)
    return out


def add_columns(ref, left, right):
    lane = lax.broadcasted_iota(jnp.int32, (NX, 128), 1)
    for z in range(NZ):
        rows = slice(z * NX, (z + 1) * NX)
        for f in range(NF):
            at = z * 16 + f
            moved = pltpu.roll(left, 128 - at, 1) if at else left
            ref[f, 0, rows, :] = ref[f, 0, rows, :] + jnp.where(lane == 0, moved, 0.0)
            shift = 127 - at
            moved = pltpu.roll(right, shift, 1) if shift else right
            ref[f, 1, rows, :] = ref[f, 1, rows, :] + jnp.where(lane == 127, moved, 0.0)


def row_of(ref, f, half, row):
    return ref[f, half, pl.ds(row, NZ, stride=NX), :]


def set_row(ref, f, half, row, value):
    ref[f, half, pl.ds(row, NZ, stride=NX), :] = value


def plane_at(z):
    start = z * NX
    return pl.ds(start if isinstance(z, int) else pl.multiple_of(start, NX), NX)


def substep_kernel(src, kap, rates, dst):
    lane = lax.broadcasted_iota(jnp.int32, (NX, 128), 1)

    def body(z, others):
        halves = [[src[g, h, plane_at(z), :] for g in range(NF)] for h in range(2)]
        for f in range(NF):
            k = kap[f]
            a, b = halves[0][f], halves[1][f]
            a_up, b_up = pltpu.roll(a, 1, 1), pltpu.roll(b, 1, 1)
            a_down, b_down = pltpu.roll(a, 127, 1), pltpu.roll(b, 127, 1)
            sides = (
                jnp.where(lane == 0, b_up, a_up) + jnp.where(lane == 127, b_down, a_down),
                jnp.where(lane == 0, a_up, b_up) + jnp.where(lane == 127, a_down, b_down),
            )
            for h in range(2):
                v = halves[h][f]
                near = pltpu.roll(v, 1, 0) + pltpu.roll(v, NX - 1, 0) + sides[h]
                for other in others:
                    near = near + src[f, h, plane_at(other), :]
                dst[f, h, plane_at(z), :] = (
                    reacted(halves[h], f, 0.5, 1.0 - 12.0 * k, rates) + (2.0 * k) * near
                )

    body(0, (1,))

    def step(z, carry):
        body(z, (z - 1, z + 1))
        return carry

    lax.fori_loop(1, NZ - 1, step, 0)
    body(NZ - 1, (NZ - 2,))


def add_ghost(dst, z, tiles, kap):
    wide = table_dot(jnp.concatenate(tiles, axis=0), spread_table())
    for f in range(NF):
        part = (2.0 * kap[f]) * wide[f * 8 : f * 8 + 8]
        for h in range(2):
            for x in range(2):
                rows = pl.ds(z * NX + x, 8, stride=2)
                dst[f, h, rows, :] = dst[f, h, rows, :] + part[:, h * 128 : (h + 1) * 128]


def is_even(axis):
    return (lax.axis_index(axis) & 1) == 0


def pick(flag, one, other):
    return jnp.where(flag, one, other)


def prep_kernel(c, u_in, u, odd, even, own, packs, sems):
    even_y = is_even("gy")
    copies = [
        pltpu.make_async_copy(u_in.at[:, :, h * 128 : (h + 1) * 128], u.at[:, h], sems.at[h])
        for h in range(2)
    ]
    for n, (slot, dst) in enumerate(((pick(even_y, 0, 2), odd), (pick(even_y, 2, 0), even), (1, own))):
        for side, k in ((0, LOW), (1, HIGH)):
            copies.append(
                pltpu.make_async_copy(
                    c.at[slot, :, k], dst.at[pl.ds(side * NF, NF)], sems.at[2 + 2 * n + side]
                )
            )
    for copy in copies:
        copy.start()
    for copy in copies[:2]:
        copy.wait()
    packed = [pack_columns(u, side) for side in range(2)]
    for t in range(2):
        left, right = (packed[side][8 * t : 8 * t + 8] for side in range(2))
        packs[t] = left
        packs[2 + t] = right
        odd[18 + t] = pick(even_y, left, right)
        even[18 + t] = pick(even_y, right, left)
    for copy in copies[2:]:
        copy.wait()


def middle_kernel(c, kap, rates, odd, even, own):
    even_y = is_even("gy")
    for slot, dst in ((pick(even_y, 0, 2), odd), (1, own), (pick(even_y, 2, 0), even)):
        for side, k in ((0, LOW), (1, HIGH)):
            tiles = [c[slot, g, k] for g in range(NF)]
            for f in range(NF):
                kf = kap[f]
                near = c[slot, f, k - 1] + c[slot, f, k + 1]
                dst[side * NF + f] = (
                    reacted(tiles, f, 0.5, 1.0 - kf, rates) + (0.5 * kf) * near
                )


def chosen(owner, odd, even, own, rims):
    mine = owner[lax.axis_index("gx"), lax.axis_index("gy")]
    at_odd = mine == pick(is_even("gy"), -1, 1)
    for t in range(18):
        rims[t] = jnp.where(mine == 0, own[t], jnp.where(at_odd, odd[t], even[t]))


def stacked(ref, at):
    return jnp.concatenate([ref[at], ref[at + 1]], axis=0)


def first_kernel(
    u, w, odd_in, even_in, own, packs, y_odd_in, y_even_in, owner, kap,
    u1, y_odd, y_even, x_odd, x_even, rims, packs1,
):
    even_y = is_even("gy")
    even_x = is_even("gx")
    chosen(owner, odd_in, even_in, own, rims)
    add_ghost(u1, 0, [rims[f] for f in range(NF)], kap)
    add_ghost(u1, NZ - 1, [rims[NF + f] for f in range(NF)], kap)
    k_lanes = kappa_lanes(kap)
    odd, even = stacked(odd_in, 18), stacked(even_in, 18)
    from_left = pick(even_y, odd, even)
    from_right = pick(even_y, even, odd)
    left = k_lanes * (from_left - stacked(packs, 2))
    right = k_lanes * (from_right - stacked(packs, 0))
    add_columns(u1, left, right)
    for f in range(NF):
        k2 = 2.0 * kap[f]
        for h in range(2):
            first = row_of(u, f, h, 0)
            last = row_of(u, f, h, NX - 1)
            new_first = row_of(u1, f, h, 0) - k2 * last
            new_last = row_of(u1, f, h, NX - 1) - k2 * first
            set_row(u1, f, h, 0, new_first)
            set_row(u1, f, h, NX - 1, new_last)
            x_odd[2 * f + h] = pick(even_x, first, last)
            x_odd[18 + 2 * f + h] = pick(even_x, new_first, new_last)
            x_even[2 * f + h] = pick(even_x, last, first)
            x_even[18 + 2 * f + h] = pick(even_x, new_last, new_first)
    facing = (from_left, from_right, stacked(packs, 0), stacked(packs, 2))
    for n, value in enumerate(facing):
        x_odd[36 + n] = pick(even_x, value[0:8], value[8:16])
        x_even[36 + n] = pick(even_x, value[8:16], value[0:8])
    packed = [pack_columns(u1, side) for side in range(2)]
    for t in range(2):
        left, right = (packed[side][8 * t : 8 * t + 8] for side in range(2))
        packs1[t] = left
        packs1[2 + t] = right
        y_odd[18 + t] = pick(even_y, left, right)
        y_even[18 + t] = pick(even_y, right, left)


def pair_rows(ref, f, half, z):
    return (
        ref[f, half, pl.ds(z * NX, 8, stride=2), :]
        + ref[f, half, pl.ds(z * NX + 1, 8, stride=2), :]
    )


def add_rows(u, u1, new, message, k_of, rates, first):
    here = pick(first, 0, NX - 1)
    inner = pick(first, 1, NX - 2)
    opposite = pick(first, NX - 1, 0)
    layer = lax.broadcasted_iota(jnp.int32, (NZ, 128), 0)
    lane = lax.broadcasted_iota(jnp.int32, (NZ, 128), 1)
    delta = [[2.0 * k_of(g) * message[2 * g + h] for g in range(NF)] for h in range(2)]
    for f in range(NF):
        k = k_of(f)
        k2 = 2.0 * k
        a, b = delta[0][f], delta[1][f]
        a_up, b_up = pltpu.roll(a, 1, 1), pltpu.roll(b, 1, 1)
        a_down, b_down = pltpu.roll(a, 127, 1), pltpu.roll(b, 127, 1)
        sides = (
            jnp.where(lane == 0, b_up, a_up) + jnp.where(lane == 127, b_down, a_down),
            jnp.where(lane == 0, a_up, b_up) + jnp.where(lane == 127, a_down, b_down),
        )
        for h in range(2):
            d = delta[h][f]
            near = sides[h] + jnp.where(layer == 0, 0.0, pltpu.roll(d, 1, 0))
            near = near + jnp.where(layer == NZ - 1, 0.0, pltpu.roll(d, NZ - 1, 0))
            halo = message[18 + 2 * f + h] + k2 * row_of(u, f, h, here)
            near = near + (halo - row_of(u1, f, h, opposite))
            more = reacted(delta[h], f, 0.5, 1.0 - 12.0 * k, rates) + k2 * near
            set_row(new, f, h, here, row_of(new, f, h, here) + more)
            set_row(new, f, h, inner, row_of(new, f, h, inner) + k2 * d)
    return delta


def second_kernel(
    u, u1, new_in, x_odd, x_even, y_odd, y_even, own_mid, packs1, old, owner, kap, rates,
    new, payload, mids, sums,
):
    even_y = is_even("gy")
    even_x = is_even("gx")
    chosen(owner, y_odd, y_even, own_mid, mids)
    add_ghost(new, 0, [mids[f] for f in range(NF)], kap)
    add_ghost(new, NZ - 1, [mids[NF + f] for f in range(NF)], kap)
    k_of = lambda f: kap[f]
    delta_odd = add_rows(u, u1, new, x_odd, k_of, rates, even_x)
    delta_even = add_rows(u, u1, new, x_even, k_of, rates, jnp.logical_not(even_x))
    k_lanes = kappa_lanes(kap)
    x_id = lax.broadcasted_iota(jnp.int32, (NX, 128), 0)

    def facing(tile):
        low = pltpu.roll(pick(even_x, x_odd[tile], x_even[tile]), 1, 0)
        high = pltpu.roll(pick(even_x, x_even[tile], x_odd[tile]), 7, 0)
        both = jnp.concatenate([low, high], axis=0)
        return k_lanes * jnp.where((x_id == 0) | (x_id == NX - 1), both, 0.0)

    odd, even = stacked(y_odd, 18), stacked(y_even, 18)
    left = pick(even_y, odd, even) + facing(36) - (stacked(packs1, 2) + facing(39))
    right = pick(even_y, even, odd) + facing(37) - (stacked(packs1, 0) + facing(38))
    add_columns(new, k_lanes * left, k_lanes * right)
    row_odd = pick(even_x, 0, 7)
    row_even = pick(even_x, 7, 0)
    row_id = lax.broadcasted_iota(jnp.int32, (8, 128), 0)
    for f in range(NF):
        for h in range(2):
            lanes = slice(h * 128, (h + 1) * 128)
            for c in range(4):
                sums[f * 6 + 1 + c, :, lanes] = pair_rows(new, f, h, 2 * c) + pair_rows(
                    new, f, h, 2 * c + 1
                )
            for at, z in ((0, 0), (5, NZ - 1)):
                pair = pair_rows(u, f, h, z) + pair_rows(u1, f, h, z)
                odd = delta_odd[h][f][z : z + 1]
                even = delta_even[h][f][z : z + 1]
                pair = pair + jnp.where(
                    row_id == row_odd, odd, jnp.where(row_id == row_even, even, 0.0)
                )
                sums[f * 6 + at, :, lanes] = pair
    table = gather_table()
    for f in range(NF):
        coarse = table_dot(sums[f * 6 : f * 6 + 6].reshape(48, NY), table)
        for c in range(4):
            payload[f * 6 + 1 + c] = coarse[8 + c * 8 : c * 8 + 16] * 0.125
        kf = kap[f]
        payload[f * 6] = kf * (old[f] + mids[f] - 0.25 * coarse[0:8])
        payload[f * 6 + 5] = kf * (0.25 * coarse[40:48] - old[9 + f] - mids[9 + f])


def used_flags(owner):
    row = lax.axis_index("gx")
    col = lax.axis_index("gy")
    size = lax.axis_size("gy")
    left = owner[row, lax.rem(col + size - 1, size)] == 1
    self_used = owner[row, col] == 0
    right = owner[row, lax.rem(col + 1, size)] == -1
    return left, self_used, right


def coarse_kernel(c, new, payload, owner, kap, rates, out, fine_out, base, full, sems):
    copies = [
        pltpu.make_async_copy(new.at[:, h], fine_out.at[:, :, h * 128 : (h + 1) * 128], sems.at[h])
        for h in range(2)
    ]
    for copy in copies:
        copy.start()
    for slot, used in enumerate(used_flags(owner)):
        for k in (0, 1, 2, 3, 8, 9, 10, 11):
            tiles = [c[slot, g, k] for g in range(NF)]
            for f in range(NF):
                kf = kap[f]
                near = None
                count = 0.0
                if k not in (0, HIGH):
                    near = c[slot, f, k - 1]
                    count += 1.0
                if k not in (LOW, 11):
                    above = c[slot, f, k + 1]
                    near = above if near is None else near + above
                    count += 1.0
                value = reacted(tiles, f, 1.0, 1.0 - count * kf, rates) + kf * near
                if k == LOW:
                    base[slot, f, 0] = value
                    if slot == 1:
                        value = value - payload[f * 6]
                if k == HIGH:
                    base[slot, f, 1] = value
                    if slot == 1:
                        value = value + payload[f * 6 + 5]
                full[slot, f, k] = jnp.where(used, value, tiles[f])
        for f in range(NF):
            for k in range(4, 8):
                value = c[slot, f, k]
                if slot == 1:
                    value = jnp.where(used, payload[f * 6 + k - 3], value)
                full[slot, f, k] = value
        copy = pltpu.make_async_copy(full.at[slot], out.at[slot], sems.at[2 + slot])
        copy.start()
        copies.append(copy)
    for copy in copies:
        copy.wait()


def finish_kernel(out_in, base, odd, even, owner, out, fixed, sems):
    flags = used_flags(owner)
    even_y = is_even("gy")
    for n, slot in enumerate((0, 2)):
        at_odd = even_y if slot == 0 else jnp.logical_not(even_y)
        for src, here in ((odd, at_odd), (even, jnp.logical_not(at_odd))):

            @pl.when(jnp.logical_and(flags[slot], here))
            def _(n=n, slot=slot, src=src):
                for f in range(NF):
                    fixed[n, f, 0] = base[slot, f, 0] - src[f, 0]
                    for k in range(1, 5):
                        fixed[n, f, k] = src[f, k]
                    fixed[n, f, 5] = base[slot, f, 1] + src[f, 5]
                pltpu.make_async_copy(
                    fixed.at[n], out.at[slot, :, LOW : HIGH + 1], sems.at[n]
                ).start()

    for n, slot in enumerate((0, 2)):

        @pl.when(flags[slot])
        def _(n=n, slot=slot):
            pltpu.make_async_copy(fixed.at[n], out.at[slot, :, LOW : HIGH + 1], sems.at[n]).wait()


def swapped(value, axis, odd):
    size = lax.axis_size(axis)
    pairs = []
    for i in range(odd, size, 2):
        j = (i + 1) % size
        pairs += [(i, j), (j, i)]
    return lax.ppermute(value, axis, pairs)


def both(odd, even, axis):
    return swapped(odd, axis, 1), swapped(even, axis, 0)


def on_device(fine_state, coarse_column_state, diffusivity, rates, owner_offset):
    fine_shape = fine_state.shape
    u_in = fine_state.reshape(NF, NZ * NX, NY)
    c = coarse_column_state
    split = (NF, 2, NZ * NX, 128)
    dma = pltpu.SemaphoreType.DMA
    u, odd, even, own, packs = call(
        prep_kernel,
        "prep",
        [split, (20, 8, 128), (20, 8, 128), (18, 8, 128), (4, 8, 128)],
        [pltpu.HBM, pltpu.HBM],
        1 << 20,
        limit=58,
        scratch=[dma((8,))],
    )(c, u_in)
    odd, even = both(odd, even, "gy")
    y_odd, y_even, own_mid = call(
        middle_kernel,
        "middle",
        [(20, 8, 128), (20, 8, 128), (18, 8, 128)],
        [VMEM, SMEM, SMEM],
        1 << 25,
    )(c, diffusivity, rates)

    def substep(v, name):
        (w,) = call(substep_kernel, name, [split], [VMEM, SMEM, SMEM], 1 << 27)(
            v, diffusivity, rates
        )
        return w

    w = substep(u, "inner1")
    u1, y_odd, y_even, x_odd, x_even, old, packs1 = call(
        first_kernel,
        "first",
        [split, (20, 8, 128), (20, 8, 128), (40, 8, 128), (40, 8, 128), (18, 8, 128), (4, 8, 128)],
        [VMEM] * 8 + [SMEM] * 2,
        1 << 26,
        aliases={1: 0, 6: 1, 7: 2},
    )(u, w, odd, even, own, packs, y_odd, y_even, owner_offset, diffusivity)
    x_odd, x_even = both(x_odd, x_even, "gx")
    y_odd, y_even = both(y_odd, y_even, "gy")
    w = substep(u1, "inner2")
    new, payload = call(
        second_kernel,
        "second",
        [split, (54, 8, 128)],
        [VMEM] * 10 + [SMEM] * 3,
        1 << 26,
        aliases={2: 0},
        scratch=[pltpu.VMEM((18, 8, 128), F32), pltpu.VMEM((54, 8, NY), F32)],
    )(
        u, u1, w, x_odd, x_even, y_odd, y_even, own_mid, packs1, old, owner_offset,
        diffusivity, rates,
    )
    odd, even = both(payload, payload, "gy")
    out, fine_new, base = call(
        coarse_kernel,
        "coarse",
        [c.shape, u_in.shape, (3, NF, 2, 8, 128)],
        [VMEM] * 3 + [SMEM] * 3,
        1 << 26,
        scratch=[pltpu.VMEM(c.shape, F32), dma((5,))],
        out_spaces=[pltpu.HBM, pltpu.HBM, VMEM],
    )(c, new, payload, owner_offset, diffusivity, rates)
    six = (NF, 6, 8, 128)
    (coarse_new,) = call(
        finish_kernel,
        "finish",
        [c.shape],
        [pltpu.HBM, VMEM, VMEM, VMEM, SMEM],
        1 << 20,
        aliases={0: 0},
        scratch=[pltpu.VMEM((2,) + six, F32), dma((2,))],
        out_spaces=[pltpu.HBM],
    )(out, base, odd.reshape(six), even.reshape(six), owner_offset)
    return fine_new.reshape(fine_shape), coarse_new


def solution(mesh):
    in_specs = (P(None, None, "gx", "gy"), P(None, None, None, "gx", "gy"), P(), P(), P())
    out_specs = (P(None, None, "gx", "gy"), P(None, None, None, "gx", "gy"))
    return jax.shard_map(
        on_device, mesh=mesh, in_specs=in_specs, out_specs=out_specs, check_vma=False
    )
```

time: 177 us -> 40.4 us (0.23)
  the two profiles are of different devices: /device:TPU:0 before, /device:TPU:1 now
where the time goes in v1:
time: 40.4 us; the launch traced here: 40 us
  starting transfers between devices  18.4 us (46%)
  Pallas kernels  14.7 us (36%)
  waiting for transfers between devices  6 us (15%)
  between operations  0.78 us (2%)
    ppermute x8, starting transfers between devices, swapped(): return lax.ppermute(value, axis, pairs)  18.4 us
    ppermute x8, waiting for transfers between devices, swapped(): return lax.ppermute(value, axis, pairs)  6 us
    pallas_call x2, Pallas kernels, substep(): call(substep_kernel, name, [split], [VMEM, SMEM, SMEM], 1 << 27)  4.2 us
    pallas_call x1, Pallas kernels, on_device(): call(prep_kernel, 'prep', [split, (20, 8, 128), (20, 8, 128), (18, 8, 128...  2.89 us
    pallas_call x1, Pallas kernels, on_device(): call(coarse_kernel, 'coarse', [c.shape, u_in.shape, (3, NF, 2, 8, 128)],...  2.54 us
    pallas_call x1, Pallas kernels, on_device(): call(second_kernel, 'second', [split, (54, 8, 128)], [VMEM] * 10 + [SMEM]...  1.96 us
    pallas_call x1, Pallas kernels, on_device(): call(first_kernel, 'first', [split, (20, 8, 128), (20, 8, 128), (40, 8, 1...  1.5 us
    pallas_call x1, Pallas kernels, on_device(): call(middle_kernel, 'middle', [(20, 8, 128), (20, 8, 128), (18, 8, 128)],...  0.89 us
  transfers between devices with their start and end apart: 8, of which 4 were waited for; matrix products, arithmetic and copies ran while one was open for 0% of the time, Pallas kernels for 19%

profile of v1, /device:TPU:1, one launch (start us, length us, event | category | flops | bytes accessed | tf_op | source)
XLA Modules:
  0.0 40.0 jit_solution(6286994982366843551)
XLA Ops:
  0.7 2.9 %prep.1 = (f32[9,2,128,128]{3,2,1,0:T(8,128)}, f32[20,8,128]{2,1,0:T(8,128)}, f32[20,8,128]{2,1,0:T(8,128)}, f32[18,8,128]{2,1,0:T(8,128)}, f32[4,8,128]{2,1,0:T(8,128)}) custom-call(f32[3,9,12,8,128]{4,3,2,1,0:T(8,128)} %c.5, f32[9,128,256]{2,1,0:T(8,128)} %bitcast.6), custom_call_target="tpu_custom_call" | custom-call | flops 1048576 | bytes 1048576 | tf_op jit(solution)/shard_map/prep/pallas_call | solution.py:441
  3.6 0.0 copy-start.1
  3.6 5.8 %collective-permute-start = (f32[20,8,128]{2,1,0:T(8,128)}, f32[20,8,128]{2,1,0:T(8,128)S(1)}, u32[]{:S(2)}, u32[]{:S(2)}) collective-permute-start(f32[20,8,128]{2,1,0:T(8,128)} %get-tuple-element.23), channel_id=1, source_target_pairs={{1,2},{2,1},{3,4},{4,3},{5,6},{6,5},{7,8},{8,7},{9,10},{10,9},{11,... | collective-permute-start | bytes 245768 | tf_op jit(solution)/shard_map/ppermute | solution.py:428
  9.4 0.0 collective-permute-start.1
  9.4 0.9 %middle.1 = (f32[20,8,128]{2,1,0:T(8,128)S(1)}, f32[20,8,128]{2,1,0:T(8,128)S(1)}, f32[18,8,128]{2,1,0:T(8,128)S(1)}) custom-call(f32[3,9,12,8,128]{4,3,2,1,0:T(8,128)S(1)} %copy-done, f32[9]{0:T(128)S(1)} %copy-done.5, f32[9,9]{1,0:T(8,128)S(1)} %copy-done.2), custom_call_target="tpu_custom_call" | custom-call | flops 33554432 | bytes 1048576 | tf_op jit(solution)/shard_map/middle/pallas_call | solution.py:451
  10.3 0.0 copy-start.3
  10.4 2.1 %inner1.1.w = f32[9,2,128,128]{3,2,1,0:T(8,128)S(1)} custom-call(f32[9,2,128,128]{3,2,1,0:T(8,128)S(1)} %copy-done.1, f32[9]{0:T(128)S(1)} %copy-done.5, f32[9,9]{1,0:T(8,128)S(1)} %copy-done.2), custom_call_target="tpu_custom_call" | custom-call | flops 134217728 | bytes 1048576 | tf_op jit(solution)/shard_map/inner1/pallas_call | solution.py:460
  12.5 0.0 collective-permute-done.odd_in
  12.5 0.7 %collective-permute-done.1.even_in = f32[20,8,128]{2,1,0:T(8,128)S(1)} collective-permute-done((f32[20,8,128]{2,1,0:T(8,128)}, f32[20,8,128]{2,1,0:T(8,128)S(1)}, u32[]{:S(2)}, u32[]{:S(2)}) %collective-permute-start.1) | collective-permute-done | bytes 81952 | tf_op jit(solution)/shard_map/ppermute | solution.py:428
  13.2 1.5 %first.1 = (f32[9,2,128,128]{3,2,1,0:T(8,128)S(1)}, f32[20,8,128]{2,1,0:T(8,128)S(1)}, f32[20,8,128]{2,1,0:T(8,128)S(1)}, f32[40,8,128]{2,1,0:T(8,128)S(1)}, f32...) custom-call(f32[9,2,128,128]{3,2,1,0:T(8,128)S(1)} %copy-done.1, ...), custom_call_target="tpu_custom_call", output_to_operand_aliasing={{0}: (1, {}), {1}: (6, {}), {2}: (7, {})} | custom-call | flops 67108864 | bytes 1048576 | tf_op jit(solution)/shard_map/first/pallas_call | solution.py:466
  14.7 3.4 %collective-permute-start.2 = (f32[40,8,128]{2,1,0:T(8,128)S(1)}, f32[40,8,128]{2,1,0:T(8,128)S(1)}, u32[]{:S(2)}, u32[]{:S(2)}) collective-permute-start(f32[40,8,128]{2,1,0:T(8,128)S(1)} %get-tuple-element.30), channel_id=1, source_target_pairs={{16,32},{32,16},{48,64},{64,48},{80,96},{96,80},{112,128},{128,112... | collective-permute-start | bytes 491528 | tf_op jit(solution)/shard_map/ppermute | solution.py:428
  18.1 2.3 %collective-permute-start.3 = (f32[40,8,128]{2,1,0:T(8,128)S(1)}, f32[40,8,128]{2,1,0:T(8,128)S(1)}, u32[]{:S(2)}, u32[]{:S(2)}) collective-permute-start(f32[40,8,128]{2,1,0:T(8,128)S(1)} %get-tuple-element.31), channel_id=1, source_target_pairs={{0,16},{16,0},{32,48},{48,32},{64,80},{80,64},{96,112},{112,96},{1... | collective-permute-start | bytes 491528 | tf_op jit(solution)/shard_map/ppermute | solution.py:428
  20.5 3.3 %collective-permute-start.4 = (f32[20,8,128]{2,1,0:T(8,128)S(1)}, f32[20,8,128]{2,1,0:T(8,128)S(1)}, u32[]{:S(2)}, u32[]{:S(2)}) collective-permute-start(f32[20,8,128]{2,1,0:T(8,128)S(1)} %get-tuple-element.32), channel_id=1, source_target_pairs={{1,2},{2,1},{3,4},{4,3},{5,6},{6,5},{7,8},{8,7},{9,10},{10,9},{11,... | collective-permute-start | bytes 245768 | tf_op jit(solution)/shard_map/ppermute | solution.py:428
  23.8 0.0 collective-permute-start.5
  23.8 2.1 %inner2.1.new_in = f32[9,2,128,128]{3,2,1,0:T(8,128)S(1)} custom-call(f32[9,2,128,128]{3,2,1,0:T(8,128)S(1)} %get-tuple-element.29.src.u1, f32[9]{0:T(128)S(1)} %copy-done.5, f32[9,9]{1,0:T(8,128)S(1)} %copy-done.2), custom_call_target="tpu_custom_call" | custom-call | flops 134217728 | bytes 1048576 | tf_op jit(solution)/shard_map/inner2/pallas_call | solution.py:460
  25.9 1.9 %collective-permute-done.4.y_odd = f32[20,8,128]{2,1,0:T(8,128)S(1)} collective-permute-done((f32[20,8,128]{2,1,0:T(8,128)S(1)}, f32[20,8,128]{2,1,0:T(8,128)S(1)}, u32[]{:S(2)}, u32[]{:S(2)}) %collective-permute-start.4) | collective-permute-done | bytes 81952 | tf_op jit(solution)/shard_map/ppermute | solution.py:428
  27.8 0.0 collective-permute-done.3.x_even
  27.8 2.0 %second.1 = (f32[9,2,128,128]{3,2,1,0:T(8,128)S(1)}, f32[54,8,128]{2,1,0:T(8,128)S(1)}) custom-call(f32[9,2,128,128]{3,2,1,0:T(8,128)S(1)} %copy-done.1, f32[9,2,128,128]{3,2,1,0:T(8,128)S(1)} %get-tuple-element.29.src.u1, f32[9,2,128,128]{3,2,1,0:T(8,128)S(1)} %inner2.1.new_in, ...), custom_call_target="tpu_custom_call", output_to_operand_aliasing={{0}: (2, {})} | custom-call | flops 67108864 | bytes 1048576 | tf_op jit(solution)/shard_map/second/pallas_call | solution.py:477
  29.8 0.1 collective-permute-start.7
  29.9 3.4 %collective-permute-start.6 = (f32[54,8,128]{2,1,0:T(8,128)S(1)}, f32[54,8,128]{2,1,0:T(8,128)S(1)}, u32[]{:S(2)}, u32[]{:S(2)}) collective-permute-start(f32[54,8,128]{2,1,0:T(8,128)S(1)} %get-tuple-element.38.payload), channel_id=1, source_target_pairs={{1,2},{2,1},{3,4},{4,3},{5,6},{6,5},{7,8},{8,7},{9,10},{10,9},{11,... | collective-permute-start | bytes 663560 | tf_op jit(solution)/shard_map/ppermute | solution.py:428
  33.3 2.5 %coarse.1 = (f32[3,9,12,8,128]{4,3,2,1,0:T(8,128)}, f32[9,128,256]{2,1,0:T(8,128)}, f32[3,9,2,8,128]{4,3,2,1,0:T(8,128)S(1)}) custom-call(f32[3,9,12,8,128]{4,3,2,1,0:T(8,128)S(1)} %copy-done, f32[9,2,128,128]{3,2,1,0:T(8,128)S(1)} %get-tuple-element.37.new, f32[54,8,128]{2,1,0:T(8,128)S(1)} %get-tuple-element.38.payload, s32[16,16]{1,0:T(8,128)S(1)} %copy-done.3, ...), custom_call_target="tpu_custom_call" | custom-call | flops 67108864 | bytes 1048576 | tf_op jit(solution)/shard_map/coarse/pallas_call | solution.py:490
  35.9 0.1 collective-permute-done.7
  36.0 3.2 %collective-permute-done.6 = f32[54,8,128]{2,1,0:T(8,128)S(1)} collective-permute-done((f32[54,8,128]{2,1,0:T(8,128)S(1)}, f32[54,8,128]{2,1,0:T(8,128)S(1)}, u32[]{:S(2)}, u32[]{:S(2)}) %collective-permute-start.6) | collective-permute-done | bytes 221216 | tf_op jit(solution)/shard_map/ppermute | solution.py:428
  39.2 0.7 %finish.1 = f32[3,9,12,8,128]{4,3,2,1,0:T(8,128)} custom-call(f32[3,9,12,8,128]{4,3,2,1,0:T(8,128)} %get-tuple-element.40.out_in, f32[3,9,2,8,128]{4,3,2,1,0:T(8,128)S(1)} %get-tuple-element.41.base, f32[9,6,8,128]{3,2,1,0:T(8,128)S(1)} %bitcast.5, f32[9,6,8,128]{3,2,1,0:T(8,128)S(1)} %bitcast.4, s32[16,16]{1,0:T(8,128)S(1)} %copy-done.3), custom_call_target="tpu_custom_call", output_to_operand_aliasing={{}: (0, {})} | custom-call | flops 1048576 | bytes 1048576 | tf_op jit(solution)/shard_map/finish/pallas_call | solution.py:500
  (14 shorter events, 0.0 us)
Async XLA Ops:
  0.6 8.8 %copy-start = (f32[3,9,12,8,128]{4,3,2,1,0:T(8,128)S(1)}, f32[3,9,12,8,128]{4,3,2,1,0:T(8,128)}, u32[]{:S(2)}) copy-start(f32[3,9,12,8,128]{4,3,2,1,0:T(8,128)} %c.5) | copy-start | bytes 3981316
  0.6 8.8 %copy-start.2 = (f32[9,9]{1,0:T(8,128)S(1)}, f32[9,9]{1,0:T(8,128)}, u32[]{:S(2)}) copy-start(f32[9,9]{1,0:T(8,128)} %rates.9) | copy-start | bytes 976
  0.7 8.8 %copy-start.5 = (f32[9]{0:T(128)S(1)}, f32[9]{0:T(128)}, u32[]{:S(2)}) copy-start(f32[9]{0:T(128)} %kap.11) | copy-start | bytes 112
  3.6 6.8 %copy-start.1 = (f32[9,2,128,128]{3,2,1,0:T(8,128)S(1)}, f32[9,2,128,128]{3,2,1,0:T(8,128)}, u32[]{:S(2)}) copy-start(f32[9,2,128,128]{3,2,1,0:T(8,128)} %get-tuple-element.22.src.u) | copy-start | bytes 3538948
  3.6 8.9 %collective-permute-start = (f32[20,8,128]{2,1,0:T(8,128)}, f32[20,8,128]{2,1,0:T(8,128)S(1)}, u32[]{:S(2)}, u32[]{:S(2)}) collective-permute-start(f32[20,8,128]{2,1,0:T(8,128)} %get-tuple-element.23), channel_id=1, source_target_pairs={{1,2},{2,1},{3,4},{4,3},{5,6},{6,5},{7,8},{8,7},{9,10},{10,9},{11,... | collective-permute-start | bytes 245768 | tf_op jit(solution)/shard_map/ppermute | solution.py:428
  9.4 3.8 %collective-permute-start.1 = (f32[20,8,128]{2,1,0:T(8,128)}, f32[20,8,128]{2,1,0:T(8,128)S(1)}, u32[]{:S(2)}, u32[]{:S(2)}) collective-permute-start(f32[20,8,128]{2,1,0:T(8,128)} %get-tuple-element.24), channel_id=1, source_target_pairs={{0,1},{1,0},{2,3},{3,2},{4,5},{5,4},{6,7},{7,6},{8,9},{9,8},{10,11... | collective-permute-start | bytes 245768 | tf_op jit(solution)/shard_map/ppermute | solution.py:428
  10.3 2.9 %copy-start.3 = (s32[16,16]{1,0:T(8,128)S(1)}, s32[16,16]{1,0:T(8,128)}, u32[]{:S(2)}) copy-start(s32[16,16]{1,0:T(8,128)} %owner.7) | copy-start | bytes 3076
  10.3 2.9 %copy-start.4 = (f32[18,8,128]{2,1,0:T(8,128)S(1)}, f32[18,8,128]{2,1,0:T(8,128)}, u32[]{:S(2)}) copy-start(f32[18,8,128]{2,1,0:T(8,128)} %get-tuple-element.25.own) | copy-start | bytes 221188
  10.4 2.9 %copy-start.6 = (f32[4,8,128]{2,1,0:T(8,128)S(1)}, f32[4,8,128]{2,1,0:T(8,128)}, u32[]{:S(2)}) copy-start(f32[4,8,128]{2,1,0:T(8,128)} %get-tuple-element.26.packs) | copy-start | bytes 49156
  14.7 13.1 %collective-permute-start.2 = (f32[40,8,128]{2,1,0:T(8,128)S(1)}, f32[40,8,128]{2,1,0:T(8,128)S(1)}, u32[]{:S(2)}, u32[]{:S(2)}) collective-permute-start(f32[40,8,128]{2,1,0:T(8,128)S(1)} %get-tuple-element.30), channel_id=1, source_target_pairs={{16,32},{32,16},{48,64},{64,48},{80,96},{96,80},{112,128},{128,112... | collective-permute-start | bytes 491528 | tf_op jit(solution)/shard_map/ppermute | solution.py:428
  18.1 9.7 %collective-permute-start.3 = (f32[40,8,128]{2,1,0:T(8,128)S(1)}, f32[40,8,128]{2,1,0:T(8,128)S(1)}, u32[]{:S(2)}, u32[]{:S(2)}) collective-permute-start(f32[40,8,128]{2,1,0:T(8,128)S(1)} %get-tuple-element.31), channel_id=1, source_target_pairs={{0,16},{16,0},{32,48},{48,32},{64,80},{80,64},{96,112},{112,96},{1... | collective-permute-start | bytes 491528 | tf_op jit(solution)/shard_map/ppermute | solution.py:428
  20.5 7.3 %collective-permute-start.4 = (f32[20,8,128]{2,1,0:T(8,128)S(1)}, f32[20,8,128]{2,1,0:T(8,128)S(1)}, u32[]{:S(2)}, u32[]{:S(2)}) collective-permute-start(f32[20,8,128]{2,1,0:T(8,128)S(1)} %get-tuple-element.32), channel_id=1, source_target_pairs={{1,2},{2,1},{3,4},{4,3},{5,6},{6,5},{7,8},{8,7},{9,10},{10,9},{11,... | collective-permute-start | bytes 245768 | tf_op jit(solution)/shard_map/ppermute | solution.py:428
  23.8 4.0 %collective-permute-start.5 = (f32[20,8,128]{2,1,0:T(8,128)S(1)}, f32[20,8,128]{2,1,0:T(8,128)S(1)}, u32[]{:S(2)}, u32[]{:S(2)}) collective-permute-start(f32[20,8,128]{2,1,0:T(8,128)S(1)} %get-tuple-element.33), channel_id=1, source_target_pairs={{0,1},{1,0},{2,3},{3,2},{4,5},{5,4},{6,7},{7,6},{8,9},{9,8},{10,11... | collective-permute-start | bytes 245768 | tf_op jit(solution)/shard_map/ppermute | solution.py:428
  29.8 6.2 %collective-permute-start.7 = (f32[54,8,128]{2,1,0:T(8,128)S(1)}, f32[54,8,128]{2,1,0:T(8,128)S(1)}, u32[]{:S(2)}, u32[]{:S(2)}) collective-permute-start(f32[54,8,128]{2,1,0:T(8,128)S(1)} %get-tuple-element.38.payload), channel_id=1, source_target_pairs={{0,1},{1,0},{2,3},{3,2},{4,5},{5,4},{6,7},{7,6},{8,9},{9,8},{10,11... | collective-permute-start | bytes 663560 | tf_op jit(solution)/shard_map/ppermute | solution.py:428
  29.9 9.3 %collective-permute-start.6 = (f32[54,8,128]{2,1,0:T(8,128)S(1)}, f32[54,8,128]{2,1,0:T(8,128)S(1)}, u32[]{:S(2)}, u32[]{:S(2)}) collective-permute-start(f32[54,8,128]{2,1,0:T(8,128)S(1)} %get-tuple-element.38.payload), channel_id=1, source_target_pairs={{1,2},{2,1},{3,4},{4,3},{5,6},{6,5},{7,8},{8,7},{9,10},{10,9},{11,... | collective-permute-start | bytes 663560 | tf_op jit(solution)/shard_map/ppermute | solution.py:428
